TPU v7x, 32 devices: a whole 2x2x4 slice. The times are simulated.
32 devices in a mesh: ctx: 8 (over y, x, core), head: 4 (over z).
Axes of the slice: x: 2, y: 2, z: 4, core: 2. Of those that a mesh axis runs over, the one named last changes fastest.
Arguments:
- queries: bfloat16 [2048, 4096], P(('ctx', 'head')), may hold values from -0.59765625 to 0.59765625
- key_in: bfloat16 [2048, 4096], P(('ctx', 'head')), may hold values from -0.59765625 to 0.59765625
- values_in: bfloat16 [2048, 4096], P(('ctx', 'head')), may hold values from -6 to 6
- strength: bfloat16 [2048, 32], P(('ctx', 'head')), may hold values from 0 to 0.95, as said below
- log_decay: bfloat16 [2048, 4096], P(('ctx', 'head')), may hold values from -1.2 to 0, as said below
- d_out: bfloat16 [2048, 4096], P(('ctx', 'head')), may hold values from -6 to 6
Outputs:
- d_queries: bfloat16 [2048, 4096], P(('ctx', 'head'))
- d_keys: bfloat16 [2048, 4096], P(('ctx', 'head'))
- d_values: bfloat16 [2048, 4096], P(('ctx', 'head'))
- d_strength: bfloat16 [2048, 32], P(('ctx', 'head'))
- d_log_decay: bfloat16 [2048, 4096], P(('ctx', 'head'))
Inputs may be any that keep to these rules, and one draw needn't show every extreme that they name: `log_decay`: every log decay is negative. Every write strength is positive and below one.
All inputs are finite; a program needn't handle non-finite values.
Results may differ from a plain program's by a relative error of at most 0.00215.
Values may be sent and summed in bfloat16 or wider, within the bound.
A program may use at most 128 MiB of HBM per device.

v0:
```python
import functools

import jax
import jax.numpy as jnp
from jax import lax
from jax.experimental import pallas as pl
from jax.experimental.pallas import tpu as pltpu
from jax.sharding import PartitionSpec as P

SPAN = 64
BASE = 8
EPS = 1e-06
F32 = jnp.float32
BF16 = jnp.bfloat16
MESH = pl.DeviceIdType.MESH

NN = (((1,), (0,)), ((), ()))
NT = (((1,), (1,)), ((), ()))


def split(x):
    high = x.astype(BF16)
    return high, (x - high.astype(F32)).astype(BF16)


def mul(a, b, dims=NN):
    return lax.dot_general(a, b, dims, preferred_element_type=F32)


def dot3(a, b, dims=NN):
    if not isinstance(a, tuple):
        return mul(a, b[0], dims) + mul(a, b[1], dims)
    if not isinstance(b, tuple):
        return mul(a[0], b, dims) + mul(a[1], b, dims)
    return mul(a[0], b[0], dims) + (mul(a[0], b[1], dims) + mul(a[1], b[0], dims))


def rows_of(pair, start, size):
    if not isinstance(pair, tuple):
        return pair[start : start + size]
    return tuple(part[start : start + size] for part in pair)


def both(a, b, axis):
    return tuple(jnp.concatenate([x, y], axis=axis) for x, y in zip(a, b))


def grids(size):
    return (
        lax.broadcasted_iota(jnp.int32, (size, size), 0),
        lax.broadcasted_iota(jnp.int32, (size, size), 1),
    )


def per_span(row_values, span, like):
    rows, width = like.shape
    return jnp.broadcast_to(row_values, (rows // span, span, width)).reshape(rows, width)


def gates(g, span):
    rows, width = g.shape
    row, col = grids(rows)
    sum_mask = jnp.where((row // span == col // span) & (col <= row), 1.0, 0.0).astype(BF16)
    gamma = mul(sum_mask, g)
    spans = gamma.reshape(rows // span, span, width)
    middle = spans[:, span // 2 - 1 : span // 2]
    end = spans[:, span - 1 : span]
    centred = gamma - per_span(middle, span, gamma)
    rise = jnp.exp(centred)
    fall = jnp.exp(-centred)
    head = rise * per_span(jnp.exp(middle), span, gamma)
    tail = fall * per_span(jnp.exp(end - middle), span, gamma)
    fade = jnp.exp(end).reshape(rows // span, width)
    return rise, fall, head, tail, fade


def column_of(table, index):
    parts, heads, share = table.shape
    row, col = grids(share)
    head = lax.broadcasted_iota(jnp.int32, (heads, share), 0)
    lines = [jnp.sum(jnp.where(head == index, table[p], 0.0), axis=0, keepdims=True) for p in range(parts)]
    return jnp.concatenate(
        [jnp.sum(jnp.where(row == col, line, 0.0), axis=1, keepdims=True) for line in lines], axis=0
    )


def norm_of(x):
    return lax.rsqrt(jnp.sum(x * x, axis=1, keepdims=True) + EPS)


def inverse(system, row, col):
    same = row // BASE == col // BASE
    near = jnp.where(same, system, 0.0)
    near_s = split(near)
    square = dot3(near_s, near_s)
    square_s = split(square)
    found = jnp.where(row == col, 1.0, 0.0) - near
    fourth = dot3(square_s, square_s)
    found = found + dot3(split(found), square_s)
    found = found + dot3(split(found), split(fourth))
    block = BASE
    while block < SPAN:
        wide = row // (2 * block) == col // (2 * block)
        off = jnp.where(wide & (row // block != col // block), system, 0.0)
        found_s = split(found)
        found = found - dot3(found_s, split(dot3(split(off), found_s)))
        block *= 2
    return found


def gatherer(n, ins, held, table_ref, table_held, send, recv, own, t_send, t_recv, t_own):
    me = lax.axis_index("head")
    heads, rows, width = held.shape[1:]
    share = rows // n
    mine = pl.ds(pl.multiple_of(me * share, share), share)

    def source(index, h, peer):
        return ins[index].at[:, pl.ds(pl.multiple_of((peer * heads + h) * width, width), width)]

    def local(index, h):
        return pltpu.make_async_copy(source(index, h, me), held.at[index, h, mine], own.at[h, index])

    def remote(index, h, step):
        peer = lax.rem(me + step, n)
        return pltpu.make_async_remote_copy(
            src_ref=source(index, h, peer), dst_ref=held.at[index, h, mine], send_sem=send.at[h, index, step],
            recv_sem=recv.at[h, index, step], device_id={"head": peer}, device_id_type=MESH,
        )

    def table_local():
        return pltpu.make_async_copy(table_ref, table_held.at[me], t_own)

    def table_remote(step):
        return pltpu.make_async_remote_copy(
            src_ref=table_ref, dst_ref=table_held.at[me], send_sem=t_send.at[step],
            recv_sem=t_recv.at[step], device_id={"head": lax.rem(me + step, n)}, device_id_type=MESH,
        )

    def start():
        for step in range(1, n):
            table_remote(step).start()

        def start_remote(h, carry):
            for index in range(len(ins)):
                for step in range(1, n):
                    remote(index, h, step).start()
            return carry

        lax.fori_loop(0, heads, start_remote, 0)
        table_local().start()

        def start_local(h, carry):
            for index in range(len(ins)):
                local(index, h).start()
            return carry

        lax.fori_loop(0, heads, start_local, 0)
        table_local().wait()
        for step in range(1, n):
            table_remote(step).wait_recv()

    def arrive(h):
        for index in range(len(ins)):
            local(index, h).wait()
            for step in range(1, n):
                remote(index, h, step).wait_recv()

    def finish():
        for step in range(1, n):
            table_remote(step).wait_send()

        def finish_head(h, carry):
            for index in range(len(ins)):
                for step in range(1, n):
                    remote(index, h, step).wait_send()
            return carry

        lax.fori_loop(0, heads, finish_head, 0)

    return start, arrive, finish


def local_part(h, span, held, table_held, saved, total_ref):
    ev_ref, ek_ref, inv_ref, a_ref, sc_ref, tr_ref, bs_ref, gs_ref = saved
    heads, rows, width = held.shape[1:]
    spans = rows // span
    k, g, q, v, o = (held[index, h] for index in range(5))
    q = q.astype(F32)
    k = k.astype(F32)
    beta = column_of(table_held[...].astype(F32), lax.axis_index("head") * heads + h)
    rise, fall, head, tail, fade = gates(g, span)
    q_unit = q * norm_of(q) * width ** (-0.5)
    k_unit = k * norm_of(k)
    row, col = grids(rows)
    inside = row // span == col // span
    k_fall_s = split(k_unit * fall)
    inner = jnp.where(inside & (col < row), dot3(split(k_unit * rise), k_fall_s, NT), 0.0)
    scores = jnp.where(inside & (col <= row), dot3(split(q_unit * rise), k_fall_s, NT), 0.0)
    a_ref[h] = inner
    sc_ref[h] = scores
    beta_row = jnp.sum(jnp.where(row == col, beta, 0.0), axis=0, keepdims=True)
    found = inverse(inner * beta_row, row, col)
    inv_ref[h] = found
    found_s = split(found)
    e_value = dot3(found_s, v)
    e_key = dot3(found_s, split(k_unit * head))
    ev_ref[h] = e_value
    ek_ref[h] = e_key
    w_key_s = split(e_key * beta)
    w_value_s = split(e_value * beta)
    reach = q_unit * head - dot3(split(scores), w_key_s)
    k_tail = k_unit * tail
    small_row, small_col = grids(width)
    diagonal = small_row == small_col
    moves, adds, backs = [], [], []
    for index in range(spans):
        at = index * span
        tail_t = split(k_tail[at : at + span].T)
        move = jnp.where(diagonal, fade[index : index + 1], 0.0) - dot3(tail_t, rows_of(w_key_s, at, span))
        add = dot3(tail_t, rows_of(w_value_s, at, span))
        back = dot3(split(reach[at : at + span].T), o[at : at + span])
        tr_ref[h, index] = move
        bs_ref[h, index] = add
        gs_ref[h, index] = back
        moves.append(move)
        adds.append(add)
        backs.append(back)
    trans, ends = moves[0], adds[0]
    grad = backs[spans - 1]
    for index in range(1, spans):
        move_s = split(moves[index])
        trans = dot3(move_s, split(trans))
        ends = dot3(move_s, split(ends)) + adds[index]
        mirror = spans - 1 - index
        grad = dot3(split(moves[mirror].T), split(grad)) + backs[mirror]
    total_ref[0, h, 0], total_ref[0, h, 1], total_ref[0, h, 2] = trans, ends, grad


def returner(n, done, db_done, outs, db_out, send, recv, own, t_send, t_recv, t_own):
    me = lax.axis_index("head")
    heads, rows, width = done.shape[1:]
    share = rows // n

    def part(peer):
        return pl.ds(pl.multiple_of(peer * share, share), share)

    def target(index, h):
        return outs[index].at[:, pl.ds(pl.multiple_of((me * heads + h) * width, width), width)]

    def local(index, h):
        return pltpu.make_async_copy(done.at[index, h, part(me)], target(index, h), own.at[h, index])

    def remote(index, h, step):
        peer = lax.rem(me + step, n)
        return pltpu.make_async_remote_copy(
            src_ref=done.at[index, h, part(peer)], dst_ref=target(index, h), send_sem=send.at[h, index, step],
            recv_sem=recv.at[h, index, step], device_id={"head": peer}, device_id_type=MESH,
        )

    def table_local():
        return pltpu.make_async_copy(db_done.at[me], db_out.at[me], t_own)

    def table_remote(step):
        peer = lax.rem(me + step, n)
        return pltpu.make_async_remote_copy(
            src_ref=db_done.at[peer], dst_ref=db_out.at[me], send_sem=t_send.at[step],
            recv_sem=t_recv.at[step], device_id={"head": peer}, device_id_type=MESH,
        )

    def emit(index, h, value):
        done[index, h] = value.astype(BF16)
        local(index, h).start()
        for step in range(1, n):
            remote(index, h, step).start()

    def finish():
        table_local().start()
        for step in range(1, n):
            table_remote(step).start()

        def finish_head(h, carry):
            for index in range(len(outs)):
                local(index, h).wait()
                for step in range(1, n):
                    remote(index, h, step).wait()
            return carry

        lax.fori_loop(0, heads, finish_head, 0)
        table_local().wait()
        for step in range(1, n):
            table_remote(step).wait()

    return emit, finish


def grad_part(h, span, held, table_held, saved, state_ref, dstate_ref, db_all, emit_head):
    ev_ref, ek_ref, inv_ref, a_ref, sc_ref, tr_ref, bs_ref, gs_ref = saved
    heads, rows, width = held.shape[1:]
    spans = rows // span
    k, g, q, _, o = (held[index, h] for index in range(5))
    q = q.astype(F32)
    k = k.astype(F32)
    beta = column_of(table_held[...].astype(F32), lax.axis_index("head") * heads + h)

    def emit(index, value):
        emit_head(index, h, value)

    rise, fall, head, tail, fade = gates(g, span)
    q_norm = norm_of(q)
    k_norm = norm_of(k)
    q_unit = q * q_norm * width ** (-0.5)
    k_unit = k * k_norm
    row, col = grids(rows)
    inside = row // span == col // span
    states = [state_ref[h]]
    grads = [dstate_ref[h]]
    for index in range(spans - 1):
        states.append(dot3(split(tr_ref[h, index]), split(states[-1])) + bs_ref[h, index])
        mirror = spans - 1 - index
        grads.insert(0, dot3(split(tr_ref[h, mirror].T), split(grads[0])) + gs_ref[h, mirror])
    states_s = [split(x) for x in states]
    grads_s = [split(x) for x in grads]

    def each(fn):
        return jnp.concatenate([fn(index, index * span) for index in range(spans)], axis=0)

    ek_s = split(ek_ref[h])
    k_tail = k_unit * tail
    k_tail_s = split(k_tail)
    error = ev_ref[h] - each(lambda i, at: dot3(rows_of(ek_s, at, span), states_s[i]))
    update_s = split(error * beta)
    d_update = dot3(split(sc_ref[h].T), o) + each(lambda i, at: dot3(rows_of(k_tail_s, at, span), grads_s[i]))
    d_value = dot3(split(inv_ref[h].T), split(d_update * beta))
    d_value_s = split(d_value)
    emit(0, d_value)
    residue = d_update - dot3(split(a_ref[h].T), d_value_s)
    d_beta = jnp.sum(error * residue, axis=1, keepdims=True)
    parts, _, share = db_all.shape
    at_row, at_col = grids(share)
    sublane = lax.broadcasted_iota(jnp.int32, (heads, share), 0)
    for p in range(parts):
        piece = d_beta[p * share : (p + 1) * share]
        line = jnp.sum(jnp.where(at_row == at_col, piece, 0.0), axis=0, keepdims=True)
        db_all[p] = jnp.where(sublane == h, line, db_all[p])
    dq_head = each(lambda i, at: dot3(o[at : at + span], states_s[i], NT))
    dk_head = -each(lambda i, at: dot3(rows_of(d_value_s, at, span), states_s[i], NT))
    dk_tail = each(lambda i, at: dot3(rows_of(update_s, at, span), grads_s[i], NT))
    d_scores = jnp.where(inside & (col <= row), dot3(o, update_s, NT), 0.0)
    d_inner = jnp.where(inside & (col < row), -dot3(d_value_s, update_s, NT), 0.0)
    k_fall_s = split(k_unit * fall)
    dq_rise = dot3(split(d_scores), k_fall_s)
    dk_rise = dot3(split(d_inner), k_fall_s)
    dk_fall = dot3(split(d_scores.T), split(q_unit * rise)) + dot3(split(d_inner.T), split(k_unit * rise))
    dq_unit = dq_rise * rise + dq_head * head
    up = dk_rise * rise + dk_head * head
    tail_part = dk_tail * tail
    down = dk_fall * fall + tail_part
    d_gamma = q_unit * dq_unit + k_unit * (up - down)
    tail_sum = jnp.sum((k_unit * tail_part).reshape(spans, span, width), axis=1, keepdims=True)
    small_row, small_col = grids(width)
    diagonal = small_row == small_col
    last = []
    for index in range(spans):
        d_fade = jnp.sum(states[index] * grads[index], axis=1, keepdims=True)
        d_fade = jnp.sum(jnp.where(diagonal, d_fade, 0.0), axis=0, keepdims=True)
        last.append(d_fade * fade[index : index + 1])
    last = jnp.concatenate([x.reshape(1, 1, width) for x in last], axis=0)
    sum_mask = jnp.where(inside & (col >= row), 1.0, 0.0).astype(BF16)
    d_decay = dot3(sum_mask, split(d_gamma)) + per_span(tail_sum + last, span, d_gamma)
    scale = width ** (-0.5)
    dq = (dq_unit - q * (q_norm * q_norm * jnp.sum(q * dq_unit, axis=1, keepdims=True))) * (q_norm * scale)
    emit(1, dq)
    dk_unit = up + down
    dk = (dk_unit - k * (k_norm * k_norm * jnp.sum(k * dk_unit, axis=1, keepdims=True))) * k_norm
    emit(2, dk)
    emit(3, d_decay)


def exchanger(total_ref, other_ref, send, recv):
    me = lax.axis_index("ctx")

    def partner(r):
        bit = 2**r
        return me + bit - 2 * bit * lax.rem(me // bit, 2)

    def swap(r, h):
        return pltpu.make_async_remote_copy(
            src_ref=total_ref.at[r, h], dst_ref=other_ref.at[r, h], send_sem=send.at[r, h],
            recv_sem=recv.at[r, h], device_id={"ctx": partner(r)}, device_id_type=MESH,
        )

    return partner, swap


def combine(r, rounds, h, total_ref, other_ref, lead_ref, trail_ref, state_ref, dstate_ref):
    upper = lax.rem(lax.axis_index("ctx") // 2**r, 2) == 1
    trans, ends, grad = (total_ref.at[r, h, index] for index in range(3))
    other, other_ends, other_grad = (other_ref.at[r, h, index] for index in range(3))
    more = r < rounds - 1

    @pl.when(upper)
    def _():
        other_s, ends_s = split(other[...]), split(other_ends[...])
        lead_s = split(lead_ref[h])
        state_ref[h] = state_ref[h] + dot3(lead_s, ends_s)
        if more:
            lead_ref[h] = dot3(lead_s, other_s)
            trans_s = split(trans[...])
            total_ref[r + 1, h, 0] = dot3(trans_s, other_s)
            total_ref[r + 1, h, 1] = dot3(trans_s, ends_s) + ends[...]
            total_ref[r + 1, h, 2] = other_grad[...] + dot3(split(other[...].T), split(grad[...]))

    @pl.when(jnp.logical_not(upper))
    def _():
        grad_s = split(other_grad[...])
        trail_s = split(trail_ref[h])
        dstate_ref[h] = dstate_ref[h] + dot3(trail_s, grad_s)
        if more:
            other_s = split(other[...])
            trail_ref[h] = dot3(trail_s, other_s, NT)
            trans_s = split(trans[...])
            total_ref[r + 1, h, 0] = dot3(other_s, trans_s)
            total_ref[r + 1, h, 1] = dot3(other_s, split(ends[...])) + other_ends[...]
            total_ref[r + 1, h, 2] = grad[...] + dot3(split(trans[...].T), grad_s)


def layer_kernel(n, rounds, span, q_ref, k_ref, v_ref, g_ref, o_ref, b_ref, dq_out, dk_out, dv_out, dg_out, db_out,
                 held, table_held, done, db_all, db_done, ev, ek, inv, a, sc, tr, bs, gs, total, other, lead, trail,
                 state, dstate, x_send, x_recv, *semaphores):
    t = pl.program_id(0)
    heads, width = held.shape[1], held.shape[3]
    saved = (ev, ek, inv, a, sc, tr, bs, gs)
    start, arrive, finish_in = gatherer(
        n, (k_ref, g_ref, q_ref, v_ref, o_ref), held, b_ref, table_held, *semaphores[:6]
    )
    emit, finish_out = returner(n, done, db_done, (dv_out, dq_out, dk_out, dg_out), db_out, *semaphores[6:])
    partner, swap = exchanger(total, other, x_send, x_recv)

    @pl.when(t == 0)
    def _():
        me = lax.axis_index("head")
        barrier = pltpu.get_barrier_semaphore()
        for step in range(1, n):
            pl.semaphore_signal(
                barrier, inc=1, device_id={"head": lax.rem(me + step, n)}, device_id_type=MESH
            )
        for r in range(rounds):
            pl.semaphore_signal(barrier, inc=1, device_id={"ctx": partner(r)}, device_id_type=MESH)
        db_all[...] = jnp.zeros_like(db_all)
        state[...] = jnp.zeros_like(state)
        dstate[...] = jnp.zeros_like(dstate)
        row, col = grids(width)
        unit = jnp.where(row == col, 1.0, 0.0)
        for h in range(heads):
            lead[h] = unit
            trail[h] = unit
        pl.semaphore_wait(barrier, n - 1 + rounds)
        start()

    def turn(r):
        h = t - 1 - r

        @pl.when((h >= 0) & (h < heads))
        def _():
            swap(r, h).wait_recv()
            combine(r, rounds, h, total, other, lead, trail, state, dstate)
            if r < rounds - 1:
                swap(r + 1, h).start()

    for r in range(rounds - 1, 0, -1):
        turn(r)

    if rounds == 1:
        turn(0)

    @pl.when(t >= rounds)
    def _():
        grad_part(t - rounds, span, held, table_held, saved, state, dstate, db_all, emit)

    if rounds > 1:
        turn(0)

    @pl.when(t < heads)
    def _():
        arrive(t)
        local_part(t, span, held, table_held, saved, total)
        swap(0, t).start()

    @pl.when(t == heads + rounds - 1)
    def _():
        db_done[...] = db_all[...].astype(BF16)
        finish_out()
        finish_in()

        def finish_swap(h, carry):
            for r in range(rounds):
                swap(r, h).wait_send()
            return carry

        lax.fori_loop(0, heads, finish_swap, 0)


def per_device(queries, key_in, values_in, strength, log_decay, d_out):
    heads_all = strength.shape[1]
    n = lax.axis_size("head")
    rounds = lax.axis_size("ctx").bit_length() - 1
    heads = heads_all // n
    width = queries.shape[1] // heads_all
    share = queries.shape[0]
    rows = n * share
    spans = rows // SPAN
    outside = pl.BlockSpec(memory_space=pl.ANY)
    full_t = jax.ShapeDtypeStruct(queries.shape, BF16)
    dma = pltpu.SemaphoreType.DMA
    vmem = pltpu.VMEM

    def semaphores(count):
        return [dma((heads, count, n))] * 2 + [dma((heads, count))] + [dma((n,))] * 2 + [dma(())]

    narrow = vmem((heads, rows, width), F32)
    square = vmem((heads, rows, rows), F32)
    state = vmem((heads, width, width), F32)
    state_list = vmem((heads, spans, width, width), F32)
    totals = vmem((rounds, heads, 3, width, width), F32)
    dq, dk, dv, dg, ds = pl.pallas_call(
        functools.partial(layer_kernel, n, rounds, SPAN),
        grid=(heads + rounds,),
        in_specs=[outside] * 6,
        out_specs=[outside] * 5,
        out_shape=[full_t] * 4 + [jax.ShapeDtypeStruct((n, heads, share), BF16)],
        scratch_shapes=[
            vmem((5, heads, rows, width), BF16), vmem((n, heads_all, share), BF16),
            vmem((4, heads, rows, width), BF16), vmem((n, heads, share), F32), vmem((n, heads, share), BF16),
        ] + [narrow] * 2 + [square] * 3 + [state_list] * 3 + [totals] * 2 + [state] * 4
        + [dma((rounds, heads))] * 2 + semaphores(5) + semaphores(4),
        compiler_params=pltpu.CompilerParams(
            dimension_semantics=("arbitrary",), vmem_limit_bytes=60 * 1024 * 1024,
            collective_id=0, has_side_effects=True,
        ),
        name="layer",
    )(queries, key_in, values_in, log_decay, d_out, strength.T)
    return dq, dk, dv, ds.reshape(heads_all, share).T, dg


def solution(mesh):
    spec = P(("ctx", "head"), None)
    return jax.shard_map(
        per_device, mesh=mesh, in_specs=(spec,) * 6, out_specs=(spec,) * 5, check_vma=False
    )
```

profile of v0, /device:TPU:0, one launch (start us, length us, event | category | flops | bytes accessed | tf_op | source)
XLA Modules:
  0.0 127.5 jit_solution(4886750240754041065)
XLA Ops:
  0.6 121.5 %layer.1 = (bf16[64,4096]{1,0:T(8,128)(2,1)}, bf16[64,4096]{1,0:T(8,128)(2,1)}, bf16[64,4096]{1,0:T(8,128)(2,1)}, bf16[64,4096]{1,0:T(8,128)(2,1)}, bf16[4,8,64]{2,1,0:T(8,128)(2,1)}) custom-call(bf16[64,4096]{1,0:T(8,128)(2,1)} %q_ref.1, bf16[64,4096]{1,0:T(8,128)(2,1)} %k_ref.1, bf16[64,4096]{1,0:T(8,128)(2,1)} %v_ref.1, bf16[64,4096]{1,0:T(8,128)(2,1)} %g_ref.1, ...), custom_call_target="tpu_custom_call" | custom-call | tf_op jit(solution)/shard_map/layer/pallas_call | solution.py:525
  122.2 0.0 copy-start.2
  122.2 1.9 %copy.16 = bf16[64,4096]{1,0:T(8,128)(2,1)} copy(bf16[64,4096]{1,0:T(8,128)(2,1)} %get-tuple-element.20) | data formatting | bytes 1048576
  124.1 0.0 copy-done.2
  124.1 0.0 copy-start.1
  124.1 0.8 copy.17
  124.9 0.4 copy-done.1
  125.4 0.0 copy-start.3
  125.4 0.0 copy-start
  125.4 0.8 copy.18
  126.2 0.0 copy-done.3
  126.2 0.6 copy.19
  126.8 0.0 copy-done
  126.8 0.8 copy.20
Async XLA Ops:
  122.2 1.9 %copy-start.2 = (bf16[64,4096]{1,0:T(8,128)(2,1)S(1)}, bf16[64,4096]{1,0:T(8,128)(2,1)}, u32[]{:S(2)}) copy-start(bf16[64,4096]{1,0:T(8,128)(2,1)} %get-tuple-element.21) | copy-start | bytes 1572868
  124.1 1.2 copy-start.1
  125.4 0.8 copy-start.3
  125.4 1.4 %copy-start = (bf16[64,4096]{1,0:T(8,128)(2,1)S(1)}, bf16[64,4096]{1,0:T(8,128)(2,1)}, u32[]{:S(2)}) copy-start(bf16[64,4096]{1,0:T(8,128)(2,1)} %get-tuple-element.24) | copy-start | bytes 1572868
where the time goes:
time: 128 us
  Pallas kernels  122 us (95%)
  local copies, waits for them, and re-layouts  5.35 us (4%)
    pallas_call x1, Pallas kernels, per_device(): pl.pallas_call(functools.partial(layer_kernel, n, rounds, SPAN), grid=(he...  122 us
    unnamed x13, local copies, waits for them, and re-layouts  5.35 us

commit v1 on v0

v1 whole, which is shorter than its diff:
```python
import functools

import jax
import jax.numpy as jnp
from jax import lax
from jax.experimental import pallas as pl
from jax.experimental.pallas import tpu as pltpu
from jax.sharding import PartitionSpec as P

GROUP = 4
BASE = 8
TILE = 16
RANGE = 80.0
EPS = 1e-06
F32 = jnp.float32
BF16 = jnp.bfloat16
MESH = pl.DeviceIdType.MESH

NN = (((1,), (0,)), ((), ()))
NT = (((1,), (1,)), ((), ()))


def split(x):
    high = x.astype(BF16)
    return high, (x - high.astype(F32)).astype(BF16)


def mul(a, b, dims=NN):
    return lax.dot_general(a, b, dims, preferred_element_type=F32)


def dot3(a, b, dims=NN):
    if not isinstance(a, tuple):
        return mul(a, b[0], dims) + mul(a, b[1], dims)
    if not isinstance(b, tuple):
        return mul(a[0], b, dims) + mul(a[1], b, dims)
    return mul(a[0], b[0], dims) + (mul(a[0], b[1], dims) + mul(a[1], b[0], dims))


def dot32(a, b):
    return dot3(split(a), split(b))


def rows_of(pair, start, size):
    if not isinstance(pair, tuple):
        return pair[start : start + size]
    return tuple(part[start : start + size] for part in pair)


def grids(size):
    return (
        lax.broadcasted_iota(jnp.int32, (size, size), 0),
        lax.broadcasted_iota(jnp.int32, (size, size), 1),
    )


def code(x):
    top = jnp.max(jnp.abs(x), axis=0, keepdims=True)
    scale = (top * 1.01 + 1e-30).astype(BF16)
    return jnp.exp(x * (RANGE / scale.astype(F32))).astype(BF16), scale


def decode(pair):
    coded, scale = pair
    return jnp.log(coded.astype(F32)) * (scale.astype(F32) * (1.0 / RANGE))


def pack(ref, pairs):
    width = ref.shape[1]
    row = lax.broadcasted_iota(jnp.int32, (TILE, width), 0)
    scales = jnp.zeros((TILE, width), F32)
    for index, (coded, scale) in enumerate(pairs):
        ref[TILE + index * width : TILE + (index + 1) * width] = coded
        scales = jnp.where(row == index, scale.astype(F32), scales)
    ref[:TILE] = scales.astype(BF16)


def unpack(ref, index):
    width = ref.shape[1]
    scales = ref[:TILE].astype(F32)
    return ref[TILE + index * width : TILE + (index + 1) * width], scales[index : index + 1]


def per_span(row_values, span, like):
    rows, width = like.shape
    return jnp.broadcast_to(row_values, (rows // span, span, width)).reshape(rows, width)


def gates(g, span):
    rows, width = g.shape
    row, col = grids(rows)
    sum_mask = jnp.where((row // span == col // span) & (col <= row), 1.0, 0.0).astype(BF16)
    gamma = mul(sum_mask, g)
    spans = gamma.reshape(rows // span, span, width)
    middle = spans[:, span // 2 - 1 : span // 2]
    end = spans[:, span - 1 : span]
    centred = gamma - per_span(middle, span, gamma)
    rise = jnp.exp(centred)
    fall = jnp.exp(-centred)
    head = rise * per_span(jnp.exp(middle), span, gamma)
    tail = fall * per_span(jnp.exp(end - middle), span, gamma)
    fade = jnp.exp(end).reshape(rows // span, width)
    return rise, fall, head, tail, fade


def columns_of(table, first, count):
    heads, share = table.shape
    row, col = grids(share)
    head = lax.broadcasted_iota(jnp.int32, (heads, share), 0)
    lines = [jnp.sum(jnp.where(head == first + j, table, 0.0), axis=0, keepdims=True) for j in range(count)]
    return jnp.concatenate(
        [jnp.sum(jnp.where(row == col, line, 0.0), axis=1, keepdims=True) for line in lines], axis=0
    )


def norm_of(x):
    return lax.rsqrt(jnp.sum(x * x, axis=1, keepdims=True) + EPS)


def inverse(system, row, col, span):
    same = row // BASE == col // BASE
    near = jnp.where(same, system, 0.0)
    near_s = split(near)
    square = dot3(near_s, near_s)
    square_s = split(square)
    found = jnp.where(row == col, 1.0, 0.0) - near
    fourth = dot3(square_s, square_s)
    found = found + dot3(split(found), square_s)
    found = found + dot3(split(found), split(fourth))
    block = BASE
    while block < span:
        wide = row // (2 * block) == col // (2 * block)
        off = jnp.where(wide & (row // block != col // block), system, 0.0)
        found_s = split(found)
        found = found - dot3(found_s, split(dot3(split(off), found_s)))
        block *= 2
    return found


def loaded(held, g):
    count, share, width = held.shape[2:]
    return [held[index, g].reshape(count * share, width) for index in range(5)]


def local_part(g, held, table, saved, tags):
    ev_ref, ek_ref, inv_ref, a_ref, sc_ref = saved
    count, span, width = held.shape[2:]
    rows = count * span
    k, g_in, q, v, o = loaded(held, g)
    q = q.astype(F32)
    k = k.astype(F32)
    beta = columns_of(table[...].astype(F32), g * count, count)
    rise, fall, head, tail, fade = gates(g_in, span)
    q_unit = q * norm_of(q) * width ** (-0.5)
    k_unit = k * norm_of(k)
    row, col = grids(rows)
    inside = row // span == col // span
    k_fall_s = split(k_unit * fall)
    inner = jnp.where(inside & (col < row), dot3(split(k_unit * rise), k_fall_s, NT), 0.0)
    scores = jnp.where(inside & (col <= row), dot3(split(q_unit * rise), k_fall_s, NT), 0.0)
    a_ref[g] = inner
    sc_ref[g] = scores
    beta_row = jnp.sum(jnp.where(row == col, beta, 0.0), axis=0, keepdims=True)
    found = inverse(inner * beta_row, row, col, span)
    inv_ref[g] = found
    found_s = split(found)
    e_value = dot3(found_s, v)
    e_key = dot3(found_s, split(k_unit * head))
    ev_ref[g] = e_value
    ek_ref[g] = e_key
    w_key_s = split(e_key * beta)
    w_value_s = split(e_value * beta)
    reach = q_unit * head - dot3(split(scores), w_key_s)
    k_tail = k_unit * tail
    small_row, small_col = grids(width)
    diagonal = small_row == small_col
    for j in range(count):
        at = j * span
        tail_t = split(k_tail[at : at + span].T)
        tags[g, j, 0] = jnp.where(diagonal, fade[j : j + 1], 0.0) - dot3(tail_t, rows_of(w_key_s, at, span))
        tags[g, j, 1] = dot3(tail_t, rows_of(w_value_s, at, span))
        tags[g, j, 2] = dot3(split(reach[at : at + span].T), o[at : at + span])


def grad_part(g, held, table, saved, ends, db_all, emit_group):
    ev_ref, ek_ref, inv_ref, a_ref, sc_ref = saved
    count, span, width = held.shape[2:]
    rows = count * span
    k, g_in, q, _, o = loaded(held, g)
    q = q.astype(F32)
    k = k.astype(F32)
    beta = columns_of(table[...].astype(F32), g * count, count)

    def emit(index, value):
        emit_group(index, g, value)

    rise, fall, head, tail, fade = gates(g_in, span)
    q_norm = norm_of(q)
    k_norm = norm_of(k)
    q_unit = q * q_norm * width ** (-0.5)
    k_unit = k * k_norm
    row, col = grids(rows)
    inside = row // span == col // span
    states = [ends[g, j, 0] for j in range(count)]
    grads = [ends[g, j, 1] for j in range(count)]
    states_s = [split(x) for x in states]
    grads_s = [split(x) for x in grads]

    def each(fn):
        return jnp.concatenate([fn(index, index * span) for index in range(count)], axis=0)

    ek_s = split(ek_ref[g])
    k_tail = k_unit * tail
    k_tail_s = split(k_tail)
    error = ev_ref[g] - each(lambda i, at: dot3(rows_of(ek_s, at, span), states_s[i]))
    update_s = split(error * beta)
    d_update = dot3(split(sc_ref[g].T), o) + each(lambda i, at: dot3(rows_of(k_tail_s, at, span), grads_s[i]))
    d_value = dot3(split(inv_ref[g].T), split(d_update * beta))
    d_value_s = split(d_value)
    emit(0, d_value)
    residue = d_update - dot3(split(a_ref[g].T), d_value_s)
    d_beta = jnp.sum(error * residue, axis=1, keepdims=True)
    at_row, at_col = grids(span)
    sublane = lax.broadcasted_iota(jnp.int32, db_all.shape, 0)
    for j in range(count):
        piece = d_beta[j * span : (j + 1) * span]
        line = jnp.sum(jnp.where(at_row == at_col, piece, 0.0), axis=0, keepdims=True)
        db_all[...] = jnp.where(sublane == g * count + j, line, db_all[...])
    dq_head = each(lambda i, at: dot3(o[at : at + span], states_s[i], NT))
    dk_head = -each(lambda i, at: dot3(rows_of(d_value_s, at, span), states_s[i], NT))
    dk_tail = each(lambda i, at: dot3(rows_of(update_s, at, span), grads_s[i], NT))
    d_scores = jnp.where(inside & (col <= row), dot3(o, update_s, NT), 0.0)
    d_inner = jnp.where(inside & (col < row), -dot3(d_value_s, update_s, NT), 0.0)
    k_fall_s = split(k_unit * fall)
    dq_rise = dot3(split(d_scores), k_fall_s)
    dk_rise = dot3(split(d_inner), k_fall_s)
    dk_fall = dot3(split(d_scores.T), split(q_unit * rise)) + dot3(split(d_inner.T), split(k_unit * rise))
    dq_unit = dq_rise * rise + dq_head * head
    up = dk_rise * rise + dk_head * head
    tail_part = dk_tail * tail
    down = dk_fall * fall + tail_part
    d_gamma = q_unit * dq_unit + k_unit * (up - down)
    tail_sum = jnp.sum((k_unit * tail_part).reshape(count, span, width), axis=1, keepdims=True)
    small_row, small_col = grids(width)
    diagonal = small_row == small_col
    last = []
    for index in range(count):
        d_fade = jnp.sum(states[index] * grads[index], axis=1, keepdims=True)
        d_fade = jnp.sum(jnp.where(diagonal, d_fade, 0.0), axis=0, keepdims=True)
        last.append(d_fade * fade[index : index + 1])
    last = jnp.concatenate([x.reshape(1, 1, width) for x in last], axis=0)
    sum_mask = jnp.where(inside & (col >= row), 1.0, 0.0).astype(BF16)
    d_decay = dot3(sum_mask, split(d_gamma)) + per_span(tail_sum + last, span, d_gamma)
    scale = width ** (-0.5)
    dq = (dq_unit - q * (q_norm * q_norm * jnp.sum(q * dq_unit, axis=1, keepdims=True))) * (q_norm * scale)
    emit(1, dq)
    dk_unit = up + down
    dk = (dk_unit - k * (k_norm * k_norm * jnp.sum(k * dk_unit, axis=1, keepdims=True))) * k_norm
    emit(2, dk)
    emit(3, d_decay)


def merged(low, high):
    low_t, low_a, low_g = low
    high_t, high_a, high_g = high
    low_t_s, high_t_s = split(low_t), split(high_t)
    return (
        dot3(high_t_s, low_t_s),
        dot3(high_t_s, split(low_a)) + high_a,
        low_g + dot3(split(low_t.T), split(high_g)),
    )


def through(transfer, add, state):
    return dot32(transfer, state) + add


def through_back(transfer, add, grad):
    return dot32(transfer.T, grad) + add


def layer_kernel(n, rounds, q_ref, k_ref, v_ref, g_ref, o_ref, b_ref, dq_out, dk_out, dv_out, dg_out, db_out,
                 held, table, done, db_all, db_done, ev, ek, inv, a, sc, tags, ends, tot, lead, trail, state, dstate,
                 red_send, red_recv, back_send, back_recv, scan_send, scan_recv, last_send, last_recv,
                 in_sem, table_sem, out_sem, db_sem, red_sems, back_sems, scan_sems):
    t = pl.program_id(0)
    groups, count, span, width = held.shape[1:]
    half = count // 2
    ups = range(half, count)
    downs = range(half)
    z = lax.axis_index("head")
    me = lax.axis_index("ctx")
    above = lax.rem(z + 1, n)
    below = lax.rem(z + n - 1, n)
    saved = (ev, ek, inv, a, sc)
    ins = (k_ref, g_ref, q_ref, v_ref, o_ref)
    outs = (dv_out, dq_out, dk_out, dg_out)

    def columns(g, j):
        return pl.ds(pl.multiple_of((g * count + j) * width, width), width)

    def load(index, g, j):
        return pltpu.make_async_copy(ins[index].at[:, columns(g, j)], held.at[index, g, j], in_sem.at[g, index, j])

    def store(index, g, j):
        return pltpu.make_async_copy(done.at[index, g, j], outs[index].at[:, columns(g, j)], out_sem.at[g, index, j])

    def reduce_copy(g, j):
        return pltpu.make_async_remote_copy(
            src_ref=red_send.at[g, j], dst_ref=red_recv.at[g, j], send_sem=red_sems.at[0, g, j],
            recv_sem=red_sems.at[1, g, j], device_id={"head": above if j >= half else below}, device_id_type=MESH,
        )

    def back_copy(g, j):
        return pltpu.make_async_remote_copy(
            src_ref=back_send.at[g, j], dst_ref=back_recv.at[g, j], send_sem=back_sems.at[0, g, j],
            recv_sem=back_sems.at[1, g, j], device_id={"head": below if j >= half else above}, device_id_type=MESH,
        )

    def partner(r):
        bit = 2**r
        return me + bit - 2 * bit * lax.rem(me // bit, 2)

    def upper(r):
        return lax.rem(me // 2**r, 2) == 1

    def scan_copy(r, g, i):
        final = r == rounds - 1
        source, target = (last_send, last_recv) if final else (scan_send.at[r], scan_recv.at[r])
        return pltpu.make_async_remote_copy(
            src_ref=source.at[g, i], dst_ref=target.at[g, i], send_sem=scan_sems.at[0, r, g, i],
            recv_sem=scan_sems.at[1, r, g, i], device_id={"ctx": partner(r)}, device_id_type=MESH,
        )

    at_end = (z == 0) | (z == n - 1)

    @pl.when(t == 0)
    def _():
        def start_load(g, carry):
            for index in range(len(ins)):
                for j in range(count):
                    load(index, g, j).start()
            return carry

        lax.fori_loop(0, groups, start_load, 0)
        pltpu.make_async_copy(b_ref, table, table_sem).start()
        barrier = pltpu.get_barrier_semaphore()

        @pl.when(z > 0)
        def _():
            pl.semaphore_signal(barrier, inc=1, device_id={"head": below}, device_id_type=MESH)

        @pl.when(z < n - 1)
        def _():
            pl.semaphore_signal(barrier, inc=1, device_id={"head": above}, device_id_type=MESH)

        for r in range(rounds):
            pl.semaphore_signal(barrier, inc=1, device_id={"ctx": partner(r)}, device_id_type=MESH)
        db_all[...] = jnp.zeros_like(db_all)
        pl.semaphore_wait(barrier, rounds + jnp.where(z > 0, 1, 0) + jnp.where(z < n - 1, 1, 0))
        pltpu.make_async_copy(b_ref, table, table_sem).wait()

    def own(g, j):
        return tuple(tags[g, j, index] for index in range(3))

    def received(g, j):
        ref = red_recv.at[g, j]
        return tuple(decode(unpack(ref, index)) for index in range(3))

    def send_reduced(g, j, values):
        pack(red_send.at[g, j], [code(x) for x in values])
        reduce_copy(g, j).start()

    def begin_scan(g, i, values):
        for index in range(3):
            tot[g, i, index] = values[index]
        send_scan(0, g, i, values)

    def send_scan(r, g, i, values):
        if r < rounds - 1:
            pack(scan_send.at[r, g, i], [code(x) for x in values])
        else:
            pack(last_send.at[g, i], [code(jnp.where(upper(r), values[2], values[1]))])
        scan_copy(r, g, i).start()

    def local_stage(g):
        for index in range(len(ins)):
            for j in range(count):
                load(index, g, j).wait()
        local_part(g, held, table, saved, tags)

        @pl.when(z == 0)
        def _():
            for j in ups:
                send_reduced(g, j, own(g, j))

        @pl.when(z == n - 1)
        def _():
            for j in downs:
                send_reduced(g, j, own(g, j))

    def reduce_stage(s, g):
        @pl.when(z == s)
        def _():
            for j in ups:
                reduce_copy(g, j).wait_recv()
                values = merged(received(g, j), own(g, j))
                if s < n - 1:
                    send_reduced(g, j, values)
                else:
                    begin_scan(g, j - half, values)

        @pl.when(z == n - 1 - s)
        def _():
            for j in downs:
                reduce_copy(g, j).wait_recv()
                values = merged(own(g, j), received(g, j))
                if s < n - 1:
                    send_reduced(g, j, values)
                else:
                    begin_scan(g, j, values)

    def scan_stage(r, g):
        more = r < rounds - 1

        @pl.when(at_end & upper(r))
        def _():
            for i in range(half):
                scan_copy(r, g, i).wait_recv()
                if more:
                    ref = scan_recv.at[r, g, i]
                    other, other_ends, other_grad = (decode(unpack(ref, index)) for index in range(3))
                else:
                    other_ends = decode(unpack(last_recv.at[g, i], 0))
                if r == 0:
                    state[g, i] = other_ends
                    dstate[g, i] = jnp.zeros((width, width), F32)
                else:
                    lead_s = split(lead[g, i])
                    state[g, i] = state[g, i] + dot3(lead_s, split(other_ends))
                if more:
                    if r == 0:
                        lead[g, i] = other
                        row, col = grids(width)
                        trail[g, i] = jnp.where(row == col, 1.0, 0.0)
                    else:
                        lead[g, i] = dot3(lead_s, split(other))
                    values = merged((other, other_ends, other_grad), tuple(tot[g, i, index] for index in range(3)))
                    for index in range(3):
                        tot[g, i, index] = values[index]
                    send_scan(r + 1, g, i, values)

        @pl.when(at_end & jnp.logical_not(upper(r)))
        def _():
            for i in range(half):
                scan_copy(r, g, i).wait_recv()
                if more:
                    ref = scan_recv.at[r, g, i]
                    other, other_ends, other_grad = (decode(unpack(ref, index)) for index in range(3))
                else:
                    other_grad = decode(unpack(last_recv.at[g, i], 0))
                if r == 0:
                    dstate[g, i] = other_grad
                    state[g, i] = jnp.zeros((width, width), F32)
                else:
                    trail_s = split(trail[g, i])
                    dstate[g, i] = dstate[g, i] + dot3(trail_s, split(other_grad))
                if more:
                    if r == 0:
                        trail[g, i] = other.T
                        row, col = grids(width)
                        lead[g, i] = jnp.where(row == col, 1.0, 0.0)
                    else:
                        trail[g, i] = dot3(trail_s, split(other), NT)
                    values = merged(tuple(tot[g, i, index] for index in range(3)), (other, other_ends, other_grad))
                    for index in range(3):
                        tot[g, i, index] = values[index]
                    send_scan(r + 1, g, i, values)

        if not more:
            @pl.when(z == n - 1)
            def _():
                for j in ups:
                    give_up(g, j, n - 1, code(state[g, j - half]), code(dstate[g, j - half]),
                            state[g, j - half], dstate[g, j - half])

            @pl.when(z == 0)
            def _():
                for j in downs:
                    give_down(g, j, 0, code(state[g, j]), code(dstate[g, j]), state[g, j], dstate[g, j])

    def give_up(g, j, level, state_pair, grad_pair, state_now, grad_now):
        own_t, _, own_g = own(g, j)
        ends[g, j, 1] = grad_now
        if level > 0:
            low_t, low_a, _ = received(g, j)
            ends[g, j, 0] = through(low_t, low_a, state_now)
            pack(back_send.at[g, j], [state_pair, code(through_back(own_t, own_g, grad_now))])
            back_copy(g, j).start()
        else:
            ends[g, j, 0] = state_now

    def give_down(g, j, level, state_pair, grad_pair, state_now, grad_now):
        own_t, own_a, _ = own(g, j)
        ends[g, j, 0] = state_now
        if level < n - 1:
            high_t, _, high_g = received(g, j)
            ends[g, j, 1] = through_back(high_t, high_g, grad_now)
            pack(back_send.at[g, j], [code(through(own_t, own_a, state_now)), grad_pair])
            back_copy(g, j).start()
        else:
            ends[g, j, 1] = grad_now

    def back_stage(b, g):
        def taken(j):
            back_copy(g, j).wait_recv()
            ref = back_recv.at[g, j]
            pairs = [unpack(ref, index) for index in range(2)]
            return pairs + [decode(pair) for pair in pairs]

        @pl.when(z == n - 1 - b)
        def _():
            for j in ups:
                give_up(g, j, n - 1 - b, *taken(j))

        @pl.when(z == b)
        def _():
            for j in downs:
                give_down(g, j, b, *taken(j))

    def emit(index, g, value):
        done[index, g] = value.astype(BF16).reshape(count, span, width)
        for j in range(count):
            store(index, g, j).start()

    def at(delay, stage):
        g = t - delay

        @pl.when((g >= 0) & (g < groups))
        def _():
            stage(g)

    scan_at = n
    back_at = scan_at + rounds - 1
    grad_at = back_at + n
    at(0, local_stage)
    at(grad_at, lambda g: grad_part(g, held, table, saved, ends, db_all, emit))
    for b in range(n - 1, 0, -1):
        at(back_at + b, functools.partial(back_stage, b))
    for r in range(rounds - 1, -1, -1):
        at(scan_at + r, functools.partial(scan_stage, r))
    for s in range(n - 1, 0, -1):
        at(s, functools.partial(reduce_stage, s))

    @pl.when(t == groups + grad_at - 1)
    def _():
        db_done[...] = db_all[...].astype(BF16)
        db_copy = pltpu.make_async_copy(db_done, db_out, db_sem)
        db_copy.start()

        def finish(g, carry):
            for index in range(len(outs)):
                for j in range(count):
                    store(index, g, j).wait()

            @pl.when(z < n - 1)
            def _():
                for j in ups:
                    reduce_copy(g, j).wait_send()
                for j in downs:
                    back_copy(g, j).wait_send()

            @pl.when(z > 0)
            def _():
                for j in downs:
                    reduce_copy(g, j).wait_send()
                for j in ups:
                    back_copy(g, j).wait_send()

            @pl.when(at_end)
            def _():
                for r in range(rounds):
                    for i in range(half):
                        scan_copy(r, g, i).wait_send()

            return carry

        lax.fori_loop(0, groups, finish, 0)
        db_copy.wait()


def per_device(queries, key_in, values_in, strength, log_decay, d_out):
    share, heads = strength.shape
    n = lax.axis_size("head")
    rounds = lax.axis_size("ctx").bit_length() - 1
    width = queries.shape[1] // heads
    count = GROUP
    half = count // 2
    groups = heads // count
    rows = count * share
    outside = pl.BlockSpec(memory_space=pl.ANY)
    full_t = jax.ShapeDtypeStruct(queries.shape, BF16)
    dma = pltpu.SemaphoreType.DMA
    vmem = pltpu.VMEM
    narrow = vmem((groups, rows, width), F32)
    square = vmem((groups, rows, rows), F32)
    state = vmem((groups, half, width, width), F32)
    reduced = vmem((groups, count, TILE + 3 * width, width), BF16)
    returned = vmem((groups, count, TILE + 2 * width, width), BF16)
    scanned = vmem((max(rounds - 1, 1), groups, half, TILE + 3 * width, width), BF16)
    final = vmem((groups, half, TILE + width, width), BF16)
    steps = groups + n + rounds - 1 + n
    dq, dk, dv, dg, ds = pl.pallas_call(
        functools.partial(layer_kernel, n, rounds),
        grid=(steps,),
        in_specs=[outside] * 6,
        out_specs=[outside] * 5,
        out_shape=[full_t] * 4 + [jax.ShapeDtypeStruct((heads, share), BF16)],
        scratch_shapes=[
            vmem((5, groups, count, share, width), BF16), vmem((heads, share), BF16),
            vmem((4, groups, count, share, width), BF16), vmem((heads, share), F32), vmem((heads, share), BF16),
        ] + [narrow] * 2 + [square] * 3 + [
            vmem((groups, count, 3, width, width), F32), vmem((groups, count, 2, width, width), F32),
            vmem((groups, half, 3, width, width), F32),
        ] + [state] * 4 + [reduced] * 2 + [returned] * 2 + [scanned] * 2 + [final] * 2 + [
            dma((groups, 5, count)), dma(()), dma((groups, 4, count)), dma(()),
            dma((2, groups, count)), dma((2, groups, count)), dma((2, rounds, groups, half)),
        ],
        compiler_params=pltpu.CompilerParams(
            dimension_semantics=("arbitrary",), vmem_limit_bytes=63 * 1024 * 1024,
            collective_id=0, has_side_effects=True,
        ),
        name="layer",
    )(queries, key_in, values_in, log_decay, d_out, strength.T)
    return dq, dk, dv, ds.T, dg


def solution(mesh):
    spec = P(("ctx", "head"), None)
    return jax.shard_map(
        per_device, mesh=mesh, in_specs=(spec,) * 6, out_specs=(spec,) * 5, check_vma=False
    )
```

time: 128 us -> 117 us (0.914)
  Pallas kernels: 122 us -> 110 us
    pallas_call x1, Pallas kernels: 122 us -> 110 us  [per_device(): pl.pallas_call(functools.partial(layer_kernel, n, rounds), grid=(steps,),...]
where the time goes in v1:
time: 117 us; the launch traced here: 116 us
  Pallas kernels  110 us (94%)
  local copies, waits for them, and re-layouts  5.35 us (5%)
    pallas_call x1, Pallas kernels, per_device(): pl.pallas_call(functools.partial(layer_kernel, n, rounds), grid=(steps,),...  110 us
    unnamed x13, local copies, waits for them, and re-layouts  5.35 us

profile of v1, /device:TPU:0, one launch (start us, length us, event | category | flops | bytes accessed | tf_op | source)
XLA Modules:
  0.0 116.3 jit_solution(2083738588233087700)
XLA Ops:
  0.6 110.3 %layer.1 = (bf16[64,4096]{1,0:T(8,128)(2,1)}, bf16[64,4096]{1,0:T(8,128)(2,1)}, bf16[64,4096]{1,0:T(8,128)(2,1)}, bf16[64,4096]{1,0:T(8,128)(2,1)}, bf16[32,64]{1,0:T(8,128)(2,1)}) custom-call(bf16[64,4096]{1,0:T(8,128)(2,1)} %q_ref.1, bf16[64,4096]{1,0:T(8,128)(2,1)} %k_ref.1, bf16[64,4096]{1,0:T(8,128)(2,1)} %v_ref.1, bf16[64,4096]{1,0:T(8,128)(2,1)} %g_ref.1, ...), custom_call_target="tpu_custom_call" | custom-call | tf_op jit(solution)/shard_map/layer/pallas_call | solution.py:613
  110.9 0.0 copy-start.2
  110.9 1.9 %copy.16 = bf16[64,4096]{1,0:T(8,128)(2,1)} copy(bf16[64,4096]{1,0:T(8,128)(2,1)} %get-tuple-element.20) | data formatting | bytes 1048576
  112.9 0.0 copy-done.2
  112.9 0.0 copy-start.1
  112.9 0.8 copy.17
  113.7 0.4 copy-done.1
  114.1 0.0 copy-start.3
  114.1 0.0 copy-start
  114.1 0.8 copy.18
  114.9 0.0 copy-done.3
  114.9 0.6 copy.19
  115.5 0.0 copy-done
  115.5 0.8 copy.20
Async XLA Ops:
  110.9 1.9 %copy-start.2 = (bf16[64,4096]{1,0:T(8,128)(2,1)S(1)}, bf16[64,4096]{1,0:T(8,128)(2,1)}, u32[]{:S(2)}) copy-start(bf16[64,4096]{1,0:T(8,128)(2,1)} %get-tuple-element.21) | copy-start | bytes 1572868
  112.9 1.2 %copy-start.1 = (bf16[64,4096]{1,0:T(8,128)(2,1)S(1)}, bf16[64,4096]{1,0:T(8,128)(2,1)}, u32[]{:S(2)}) copy-start(bf16[64,4096]{1,0:T(8,128)(2,1)} %get-tuple-element.22) | copy-start | bytes 1572868
  114.1 0.8 copy-start.3
  114.1 1.4 %copy-start = (bf16[64,4096]{1,0:T(8,128)(2,1)S(1)}, bf16[64,4096]{1,0:T(8,128)(2,1)}, u32[]{:S(2)}) copy-start(bf16[64,4096]{1,0:T(8,128)(2,1)} %get-tuple-element.24) | copy-start | bytes 1572868

commit v2 on v1

--- a/solution.py
+++ b/solution.py
@@ -7,8 +7,14 @@
 from jax.experimental.pallas import tpu as pltpu
 from jax.sharding import PartitionSpec as P
 
-GROUP = 4
-BASE = 8
+GROUP = 2
+HOP = 3
+SWAP = 4
+NEAR = 2
+EVERY = 2
+BACK = 4
+BATCH = 4
+BASE = 2
 TILE = 16
 RANGE = 80.0
 EPS = 1e-06
@@ -117,147 +123,201 @@
     return lax.rsqrt(jnp.sum(x * x, axis=1, keepdims=True) + EPS)
 
 
-def inverse(system, row, col, span):
-    same = row // BASE == col // BASE
-    near = jnp.where(same, system, 0.0)
-    near_s = split(near)
-    square = dot3(near_s, near_s)
-    square_s = split(square)
-    found = jnp.where(row == col, 1.0, 0.0) - near
-    fourth = dot3(square_s, square_s)
-    found = found + dot3(split(found), square_s)
-    found = found + dot3(split(found), split(fourth))
+def inverses(systems, row, col, span):
+    unit = jnp.where(row == col, 1.0, 0.0)
+    founds = [unit - jnp.where(row // BASE == col // BASE, x, 0.0) for x in systems]
     block = BASE
     while block < span:
-        wide = row // (2 * block) == col // (2 * block)
-        off = jnp.where(wide & (row // block != col // block), system, 0.0)
-        found_s = split(found)
-        found = found - dot3(found_s, split(dot3(split(off), found_s)))
+        off = (row // (2 * block) == col // (2 * block)) & (row // block != col // block)
+        lows = [x.astype(BF16) for x in founds]
+        inner = [mul(jnp.where(off, x, 0.0).astype(BF16), y) for x, y in zip(systems, lows)]
+        founds = [x - mul(y, z.astype(BF16)) for x, y, z in zip(founds, lows, inner)]
         block *= 2
-    return found
-
-
-def loaded(held, g):
-    count, share, width = held.shape[2:]
-    return [held[index, g].reshape(count * share, width) for index in range(5)]
-
-
-def local_part(g, held, table, saved, tags):
+    lows = [x.astype(BF16) for x in founds]
+    rests = [unit - y.astype(F32) - dot3(split(x), y) for x, y in zip(systems, lows)]
+    small = [x.astype(BF16) for x in rests]
+    rests = [x + mul(y, y) for x, y in zip(rests, small)]
+    return [y.astype(F32) + mul(y, x.astype(BF16)) for x, y in zip(rests, lows)]
+
+
+def loaded(held, index, batch, units, count):
+    width = held.shape[3] // (units * count)
+
+    def head(h):
+        return held[index, batch, :, h * width : (h + 1) * width]
+
+    return [jnp.concatenate([head(u * count + j) for j in range(count)], axis=0) for u in range(units)]
+
+
+def over(fn, *lists):
+    return [fn(*values) for values in zip(*lists)]
+
+
+def local_part(batch, units, count, held, table, saved, tags):
     ev_ref, ek_ref, inv_ref, a_ref, sc_ref = saved
-    count, span, width = held.shape[2:]
+    span = held.shape[2]
+    width = held.shape[3] // (units * count)
     rows = count * span
-    k, g_in, q, v, o = loaded(held, g)
-    q = q.astype(F32)
-    k = k.astype(F32)
-    beta = columns_of(table[...].astype(F32), g * count, count)
-    rise, fall, head, tail, fade = gates(g_in, span)
-    q_unit = q * norm_of(q) * width ** (-0.5)
-    k_unit = k * norm_of(k)
+    first = batch * units
+    ks, gs, qs, vs, os = (loaded(held, index, batch, units, count) for index in range(5))
+    betas = columns_of(table[...].astype(F32), first * count, units * count)
+    betas = [betas[u * rows : (u + 1) * rows] for u in range(units)]
+    qs = over(lambda x: x.astype(F32), qs)
+    ks = over(lambda x: x.astype(F32), ks)
+    rises, falls, heads, tails, fades = zip(*(gates(x, span) for x in gs))
+    q_units = over(lambda q: q * norm_of(q) * width ** (-0.5), qs)
+    k_units = over(lambda k: k * norm_of(k), ks)
     row, col = grids(rows)
     inside = row // span == col // span
-    k_fall_s = split(k_unit * fall)
-    inner = jnp.where(inside & (col < row), dot3(split(k_unit * rise), k_fall_s, NT), 0.0)
-    scores = jnp.where(inside & (col <= row), dot3(split(q_unit * rise), k_fall_s, NT), 0.0)
-    a_ref[g] = inner
-    sc_ref[g] = scores
-    beta_row = jnp.sum(jnp.where(row == col, beta, 0.0), axis=0, keepdims=True)
-    found = inverse(inner * beta_row, row, col, span)
-    inv_ref[g] = found
-    found_s = split(found)
-    e_value = dot3(found_s, v)
-    e_key = dot3(found_s, split(k_unit * head))
-    ev_ref[g] = e_value
-    ek_ref[g] = e_key
-    w_key_s = split(e_key * beta)
-    w_value_s = split(e_value * beta)
-    reach = q_unit * head - dot3(split(scores), w_key_s)
-    k_tail = k_unit * tail
+    k_falls = over(lambda k, fall: split(k * fall), k_units, falls)
+    inners = over(
+        lambda k, rise, k_fall: jnp.where(inside & (col < row), dot3(split(k * rise), k_fall, NT), 0.0),
+        k_units, rises, k_falls,
+    )
+    beta_rows = over(lambda x: jnp.sum(jnp.where(row == col, x, 0.0), axis=0, keepdims=True), betas)
+    systems = over(lambda inner, beta: inner * beta, inners, beta_rows)
+    scores = over(
+        lambda q, rise, k_fall: jnp.where(inside & (col <= row), dot3(split(q * rise), k_fall, NT), 0.0),
+        q_units, rises, k_falls,
+    )
+    founds = inverses(systems, row, col, span)
+    founds_s = over(split, founds)
+    e_keys = over(lambda x, k, head: dot3(x, split(k * head)), founds_s, k_units, heads)
+    e_values = over(dot3, founds_s, vs)
+    w_keys = over(lambda x, beta: split(x * beta), e_keys, betas)
+    w_values = over(lambda x, beta: split(x * beta), e_values, betas)
+    reaches = over(lambda q, head, score, w: q * head - dot3(split(score), w), q_units, heads, scores, w_keys)
+    k_tails = over(lambda k, tail: k * tail, k_units, tails)
     small_row, small_col = grids(width)
     diagonal = small_row == small_col
+    for u in range(units):
+        g = first + u
+        a_ref[g] = inners[u]
+        sc_ref[g] = scores[u]
+        inv_ref[g] = founds[u]
+        ev_ref[g] = e_values[u]
+        ek_ref[g] = e_keys[u]
     for j in range(count):
         at = j * span
-        tail_t = split(k_tail[at : at + span].T)
-        tags[g, j, 0] = jnp.where(diagonal, fade[j : j + 1], 0.0) - dot3(tail_t, rows_of(w_key_s, at, span))
-        tags[g, j, 1] = dot3(tail_t, rows_of(w_value_s, at, span))
-        tags[g, j, 2] = dot3(split(reach[at : at + span].T), o[at : at + span])
-
-
-def grad_part(g, held, table, saved, ends, db_all, emit_group):
+        tails_t = over(lambda x: split(x[at : at + span].T), k_tails)
+        reaches_t = over(lambda x: split(x[at : at + span].T), reaches)
+        for u in range(units):
+            g = first + u
+            tags[g, j, 0] = jnp.where(diagonal, fades[u][j : j + 1], 0.0) - dot3(tails_t[u], rows_of(w_keys[u], at, span))
+            tags[g, j, 1] = dot3(tails_t[u], rows_of(w_values[u], at, span))
+            tags[g, j, 2] = dot3(reaches_t[u], os[u][at : at + span])
+
+
+def grad_part(batch, units, count, held, table, saved, ends, db_all, done):
     ev_ref, ek_ref, inv_ref, a_ref, sc_ref = saved
-    count, span, width = held.shape[2:]
+    span = held.shape[2]
+    width = held.shape[3] // (units * count)
     rows = count * span
-    k, g_in, q, _, o = loaded(held, g)
-    q = q.astype(F32)
-    k = k.astype(F32)
-    beta = columns_of(table[...].astype(F32), g * count, count)
-
-    def emit(index, value):
-        emit_group(index, g, value)
-
-    rise, fall, head, tail, fade = gates(g_in, span)
-    q_norm = norm_of(q)
-    k_norm = norm_of(k)
-    q_unit = q * q_norm * width ** (-0.5)
-    k_unit = k * k_norm
+    first = batch * units
+    spans = range(count)
+    ks, gs, qs, _, os = (loaded(held, index, batch, units, count) for index in range(5))
+    betas = columns_of(table[...].astype(F32), first * count, units * count)
+    betas = [betas[u * rows : (u + 1) * rows] for u in range(units)]
+    numbers = [first + u for u in range(units)]
+    states = [[ends[g, j, 0] for j in spans] for g in numbers]
+    grads = [[ends[g, j, 1] for j in spans] for g in numbers]
+    scores_t = [sc_ref[g].T for g in numbers]
+    inner_t = [a_ref[g].T for g in numbers]
+    found_t = [inv_ref[g].T for g in numbers]
+    e_values = [ev_ref[g] for g in numbers]
+    e_keys = [ek_ref[g] for g in numbers]
+
+    def emit(index, values):
+        for u, value in enumerate(values):
+            for j in spans:
+                at = (u * count + j) * width
+                done[index, batch, :, at : at + width] = value[j * span : (j + 1) * span].astype(BF16)
+
+    qs = over(lambda x: x.astype(F32), qs)
+    ks = over(lambda x: x.astype(F32), ks)
+    rises, falls, heads, tails, fades = zip(*(gates(x, span) for x in gs))
+    q_norms = over(norm_of, qs)
+    k_norms = over(norm_of, ks)
+    q_units = over(lambda q, norm: q * norm * width ** (-0.5), qs, q_norms)
+    k_units = over(lambda k, norm: k * norm, ks, k_norms)
     row, col = grids(rows)
     inside = row // span == col // span
-    states = [ends[g, j, 0] for j in range(count)]
-    grads = [ends[g, j, 1] for j in range(count)]
-    states_s = [split(x) for x in states]
-    grads_s = [split(x) for x in grads]
+    states_s = [over(split, x) for x in states]
+    grads_s = [over(split, x) for x in grads]
 
     def each(fn):
-        return jnp.concatenate([fn(index, index * span) for index in range(count)], axis=0)
-
-    ek_s = split(ek_ref[g])
-    k_tail = k_unit * tail
-    k_tail_s = split(k_tail)
-    error = ev_ref[g] - each(lambda i, at: dot3(rows_of(ek_s, at, span), states_s[i]))
-    update_s = split(error * beta)
-    d_update = dot3(split(sc_ref[g].T), o) + each(lambda i, at: dot3(rows_of(k_tail_s, at, span), grads_s[i]))
-    d_value = dot3(split(inv_ref[g].T), split(d_update * beta))
-    d_value_s = split(d_value)
-    emit(0, d_value)
-    residue = d_update - dot3(split(a_ref[g].T), d_value_s)
-    d_beta = jnp.sum(error * residue, axis=1, keepdims=True)
+        return jnp.concatenate([fn(j, j * span) for j in spans], axis=0)
+
+    def cut(x, at):
+        return rows_of(x, at, span)
+
+    e_keys = over(split, e_keys)
+    k_tails = over(lambda k, tail: split(k * tail), k_units, tails)
+    errors = over(lambda ev, ek, state: ev - each(lambda j, at: dot3(cut(ek, at), state[j])), e_values, e_keys, states_s)
+    updates = over(lambda x, beta: split(x * beta), errors, betas)
+    d_updates = over(
+        lambda score, o, tail, grad: dot3(split(score), o) + each(lambda j, at: dot3(cut(tail, at), grad[j])),
+        scores_t, os, k_tails, grads_s,
+    )
+    d_values = over(lambda x, d, beta: dot3(split(x), split(d * beta)), found_t, d_updates, betas)
+    emit(0, d_values)
+    d_values = over(split, d_values)
+    residues = over(lambda d, a, value: d - dot3(split(a), value), d_updates, inner_t, d_values)
+    d_betas = over(lambda x, y: jnp.sum(x * y, axis=1, keepdims=True), errors, residues)
     at_row, at_col = grids(span)
     sublane = lax.broadcasted_iota(jnp.int32, db_all.shape, 0)
-    for j in range(count):
-        piece = d_beta[j * span : (j + 1) * span]
-        line = jnp.sum(jnp.where(at_row == at_col, piece, 0.0), axis=0, keepdims=True)
-        db_all[...] = jnp.where(sublane == g * count + j, line, db_all[...])
-    dq_head = each(lambda i, at: dot3(o[at : at + span], states_s[i], NT))
-    dk_head = -each(lambda i, at: dot3(rows_of(d_value_s, at, span), states_s[i], NT))
-    dk_tail = each(lambda i, at: dot3(rows_of(update_s, at, span), grads_s[i], NT))
-    d_scores = jnp.where(inside & (col <= row), dot3(o, update_s, NT), 0.0)
-    d_inner = jnp.where(inside & (col < row), -dot3(d_value_s, update_s, NT), 0.0)
-    k_fall_s = split(k_unit * fall)
-    dq_rise = dot3(split(d_scores), k_fall_s)
-    dk_rise = dot3(split(d_inner), k_fall_s)
-    dk_fall = dot3(split(d_scores.T), split(q_unit * rise)) + dot3(split(d_inner.T), split(k_unit * rise))
-    dq_unit = dq_rise * rise + dq_head * head
-    up = dk_rise * rise + dk_head * head
-    tail_part = dk_tail * tail
-    down = dk_fall * fall + tail_part
-    d_gamma = q_unit * dq_unit + k_unit * (up - down)
-    tail_sum = jnp.sum((k_unit * tail_part).reshape(count, span, width), axis=1, keepdims=True)
+    table_now = db_all[...]
+    for u in range(units):
+        for j in spans:
+            piece = d_betas[u][j * span : (j + 1) * span]
+            line = jnp.sum(jnp.where(at_row == at_col, piece, 0.0), axis=0, keepdims=True)
+            table_now = jnp.where(sublane == (first + u) * count + j, line, table_now)
+    db_all[...] = table_now
+    dq_heads = over(lambda o, state: each(lambda j, at: dot3(cut(o, at), state[j], NT)), os, states_s)
+    dk_heads = over(lambda d, state: -each(lambda j, at: dot3(cut(d, at), state[j], NT)), d_values, states_s)
+    dk_tails = over(lambda x, grad: each(lambda j, at: dot3(cut(x, at), grad[j], NT)), updates, grads_s)
+    d_scores = over(lambda o, x: jnp.where(inside & (col <= row), dot3(o, x, NT), 0.0), os, updates)
+    d_inners = over(lambda d, x: jnp.where(inside & (col < row), -dot3(d, x, NT), 0.0), d_values, updates)
+    k_falls = over(lambda k, fall: split(k * fall), k_units, falls)
+    dq_rises = over(lambda x, y: dot3(split(x), y), d_scores, k_falls)
+    dk_rises = over(lambda x, y: dot3(split(x), y), d_inners, k_falls)
+    dk_falls = over(
+        lambda x, y, q, k, rise: dot3(split(x.T), split(q * rise)) + dot3(split(y.T), split(k * rise)),
+        d_scores, d_inners, q_units, k_units, rises,
+    )
+    dq_units = over(lambda x, rise, y, head: x * rise + y * head, dq_rises, rises, dq_heads, heads)
+    ups = over(lambda x, rise, y, head: x * rise + y * head, dk_rises, rises, dk_heads, heads)
+    tail_parts = over(lambda x, tail: x * tail, dk_tails, tails)
+    downs = over(lambda x, fall, y: x * fall + y, dk_falls, falls, tail_parts)
+    d_gammas = over(lambda q, dq, k, up, down: q * dq + k * (up - down), q_units, dq_units, k_units, ups, downs)
+    tail_sums = over(lambda k, x: jnp.sum((k * x).reshape(count, span, width), axis=1, keepdims=True), k_units, tail_parts)
     small_row, small_col = grids(width)
     diagonal = small_row == small_col
-    last = []
-    for index in range(count):
-        d_fade = jnp.sum(states[index] * grads[index], axis=1, keepdims=True)
-        d_fade = jnp.sum(jnp.where(diagonal, d_fade, 0.0), axis=0, keepdims=True)
-        last.append(d_fade * fade[index : index + 1])
-    last = jnp.concatenate([x.reshape(1, 1, width) for x in last], axis=0)
+
+    def at_last(state, grad, fade):
+        last = []
+        for j in spans:
+            d_fade = jnp.sum(state[j] * grad[j], axis=1, keepdims=True)
+            d_fade = jnp.sum(jnp.where(diagonal, d_fade, 0.0), axis=0, keepdims=True)
+            last.append((d_fade * fade[j : j + 1]).reshape(1, 1, width))
+        return jnp.concatenate(last, axis=0)
+
+    lasts = over(at_last, states, grads, fades)
     sum_mask = jnp.where(inside & (col >= row), 1.0, 0.0).astype(BF16)
-    d_decay = dot3(sum_mask, split(d_gamma)) + per_span(tail_sum + last, span, d_gamma)
+    d_decays = over(
+        lambda x, tail, last: dot3(sum_mask, split(x)) + per_span(tail + last, span, x), d_gammas, tail_sums, lasts
+    )
     scale = width ** (-0.5)
-    dq = (dq_unit - q * (q_norm * q_norm * jnp.sum(q * dq_unit, axis=1, keepdims=True))) * (q_norm * scale)
-    emit(1, dq)
-    dk_unit = up + down
-    dk = (dk_unit - k * (k_norm * k_norm * jnp.sum(k * dk_unit, axis=1, keepdims=True))) * k_norm
-    emit(2, dk)
-    emit(3, d_decay)
+    emit(1, over(
+        lambda d, q, norm: (d - q * (norm * norm * jnp.sum(q * d, axis=1, keepdims=True))) * (norm * scale),
+        dq_units, qs, q_norms,
+    ))
+    dk_units = over(lambda x, y: x + y, ups, downs)
+    emit(2, over(
+        lambda d, k, norm: (d - k * (norm * norm * jnp.sum(k * d, axis=1, keepdims=True))) * norm,
+        dk_units, ks, k_norms,
+    ))
+    emit(3, d_decays)
 
 
 def merged(low, high):
@@ -279,12 +339,24 @@
     return dot32(transfer.T, grad) + add
 
 
+def schedule(n, rounds):
+    reduce_at = [HOP * s for s in range(n)]
+    scan_at = []
+    for r in range(rounds):
+        near = r == 0 or r == rounds - 1
+        scan_at.append((scan_at[-1] if r else reduce_at[-1]) + (NEAR if near else SWAP))
+    back_at = [scan_at[-1] + BACK * b for b in range(n)]
+    return reduce_at, scan_at, back_at, back_at[-1] + 1
+
+
 def layer_kernel(n, rounds, q_ref, k_ref, v_ref, g_ref, o_ref, b_ref, dq_out, dk_out, dv_out, dg_out, db_out,
                  held, table, done, db_all, db_done, ev, ek, inv, a, sc, tags, ends, tot, lead, trail, state, dstate,
                  red_send, red_recv, back_send, back_recv, scan_send, scan_recv, last_send, last_recv,
                  in_sem, table_sem, out_sem, db_sem, red_sems, back_sems, scan_sems):
     t = pl.program_id(0)
-    groups, count, span, width = held.shape[1:]
+    groups, count, _, width, _ = tags.shape
+    batches = held.shape[1]
+    units = groups // batches
     half = count // 2
     ups = range(half, count)
     downs = range(half)
@@ -296,14 +368,15 @@
     ins = (k_ref, g_ref, q_ref, v_ref, o_ref)
     outs = (dv_out, dq_out, dk_out, dg_out)
 
-    def columns(g, j):
-        return pl.ds(pl.multiple_of((g * count + j) * width, width), width)
-
-    def load(index, g, j):
-        return pltpu.make_async_copy(ins[index].at[:, columns(g, j)], held.at[index, g, j], in_sem.at[g, index, j])
-
-    def store(index, g, j):
-        return pltpu.make_async_copy(done.at[index, g, j], outs[index].at[:, columns(g, j)], out_sem.at[g, index, j])
+    def columns(batch):
+        size = units * count * width
+        return pl.ds(pl.multiple_of(batch * size, size), size)
+
+    def load(index, batch):
+        return pltpu.make_async_copy(ins[index].at[:, columns(batch)], held.at[index, batch], in_sem.at[batch, index])
+
+    def store(index, batch):
+        return pltpu.make_async_copy(done.at[index, batch], outs[index].at[:, columns(batch)], out_sem.at[batch, index])
 
     def reduce_copy(g, j):
         return pltpu.make_async_remote_copy(
@@ -336,13 +409,12 @@
 
     @pl.when(t == 0)
     def _():
-        def start_load(g, carry):
+        def start_load(batch, carry):
             for index in range(len(ins)):
-                for j in range(count):
-                    load(index, g, j).start()
+                load(index, batch).start()
             return carry
 
-        lax.fori_loop(0, groups, start_load, 0)
+        lax.fori_loop(0, batches, start_load, 0)
         pltpu.make_async_copy(b_ref, table, table_sem).start()
         barrier = pltpu.get_barrier_semaphore()
 
@@ -383,21 +455,27 @@
             pack(last_send.at[g, i], [code(jnp.where(upper(r), values[2], values[1]))])
         scan_copy(r, g, i).start()
 
-    def local_stage(g):
+    def local_stage(batch):
         for index in range(len(ins)):
-            for j in range(count):
-                load(index, g, j).wait()
-        local_part(g, held, table, saved, tags)
+            load(index, batch).wait()
+        local_part(batch, units, count, held, table, saved, tags)
 
         @pl.when(z == 0)
         def _():
-            for j in ups:
-                send_reduced(g, j, own(g, j))
+            for u in range(units):
+                for j in ups:
+                    send_reduced(batch * units + u, j, own(batch * units + u, j))
 
         @pl.when(z == n - 1)
         def _():
-            for j in downs:
-                send_reduced(g, j, own(g, j))
+            for u in range(units):
+                for j in downs:
+                    send_reduced(batch * units + u, j, own(batch * units + u, j))
+
+    def grad_stage(batch):
+        grad_part(batch, units, count, held, table, saved, ends, db_all, done)
+        for index in range(len(outs)):
+            store(index, batch).start()
 
     def reduce_stage(s, g):
         @pl.when(z == s)
@@ -528,11 +606,6 @@
             for j in downs:
                 give_down(g, j, b, *taken(j))
 
-    def emit(index, g, value):
-        done[index, g] = value.astype(BF16).reshape(count, span, width)
-        for j in range(count):
-            store(index, g, j).start()
-
     def at(delay, stage):
         g = t - delay
 
@@ -540,17 +613,25 @@
         def _():
             stage(g)
 
-    scan_at = n
-    back_at = scan_at + rounds - 1
-    grad_at = back_at + n
-    at(0, local_stage)
-    at(grad_at, lambda g: grad_part(g, held, table, saved, ends, db_all, emit))
+    reduce_at, scan_at, back_at, grad_at = schedule(n, rounds)
+    def at_batch(delay, stage):
+        batch = (t - delay) // units
+
+        @pl.when((t >= delay) & (lax.rem(t - delay + units, units) == 0) & (batch < batches))
+        def _():
+            stage(batch)
+
+    @pl.when((lax.rem(t, EVERY) == 0) & (t < batches * EVERY))
+    def _():
+        local_stage(t // EVERY)
+
+    at_batch(grad_at + units - 1, grad_stage)
     for b in range(n - 1, 0, -1):
-        at(back_at + b, functools.partial(back_stage, b))
+        at(back_at[b], functools.partial(back_stage, b))
     for r in range(rounds - 1, -1, -1):
-        at(scan_at + r, functools.partial(scan_stage, r))
+        at(scan_at[r], functools.partial(scan_stage, r))
     for s in range(n - 1, 0, -1):
-        at(s, functools.partial(reduce_stage, s))
+        at(reduce_at[s], functools.partial(reduce_stage, s))
 
     @pl.when(t == groups + grad_at - 1)
     def _():
@@ -559,10 +640,6 @@
         db_copy.start()
 
         def finish(g, carry):
-            for index in range(len(outs)):
-                for j in range(count):
-                    store(index, g, j).wait()
-
             @pl.when(z < n - 1)
             def _():
                 for j in ups:
@@ -586,6 +663,13 @@
             return carry
 
         lax.fori_loop(0, groups, finish, 0)
+
+        def finish_batch(batch, carry):
+            for index in range(len(outs)):
+                store(index, batch).wait()
+            return carry
+
+        lax.fori_loop(0, batches, finish_batch, 0)
         db_copy.wait()
 
 
@@ -597,6 +681,7 @@
     count = GROUP
     half = count // 2
     groups = heads // count
+    batches = groups // BATCH
     rows = count * share
     outside = pl.BlockSpec(memory_space=pl.ANY)
     full_t = jax.ShapeDtypeStruct(queries.shape, BF16)
@@ -609,7 +694,7 @@
     returned = vmem((groups, count, TILE + 2 * width, width), BF16)
     scanned = vmem((max(rounds - 1, 1), groups, half, TILE + 3 * width, width), BF16)
     final = vmem((groups, half, TILE + width, width), BF16)
-    steps = groups + n + rounds - 1 + n
+    steps = groups + schedule(n, rounds)[-1]
     dq, dk, dv, dg, ds = pl.pallas_call(
         functools.partial(layer_kernel, n, rounds),
         grid=(steps,),
@@ -617,13 +702,13 @@
         out_specs=[outside] * 5,
         out_shape=[full_t] * 4 + [jax.ShapeDtypeStruct((heads, share), BF16)],
         scratch_shapes=[
-            vmem((5, groups, count, share, width), BF16), vmem((heads, share), BF16),
-            vmem((4, groups, count, share, width), BF16), vmem((heads, share), F32), vmem((heads, share), BF16),
+            vmem((5, batches, share, BATCH * count * width), BF16), vmem((heads, share), BF16),
+            vmem((4, batches, share, BATCH * count * width), BF16), vmem((heads, share), F32), vmem((heads, share), BF16),
         ] + [narrow] * 2 + [square] * 3 + [
             vmem((groups, count, 3, width, width), F32), vmem((groups, count, 2, width, width), F32),
             vmem((groups, half, 3, width, width), F32),
         ] + [state] * 4 + [reduced] * 2 + [returned] * 2 + [scanned] * 2 + [final] * 2 + [
-            dma((groups, 5, count)), dma(()), dma((groups, 4, count)), dma(()),
+            dma((batches, 5)), dma(()), dma((batches, 4)), dma(()),
             dma((2, groups, count)), dma((2, groups, count)), dma((2, rounds, groups, half)),
         ],
         compiler_params=pltpu.CompilerParams(

time: 117 us -> 101 us (0.86)
  Pallas kernels: 110 us -> 94.5 us
    pallas_call x1, Pallas kernels: 110 us -> 94.5 us  [per_device(): pl.pallas_call(functools.partial(layer_kernel, n, rounds), grid=(steps,),...]
where the time goes in v2:
time: 101 us; the launch traced here: 100 us
  Pallas kernels  94.5 us (94%)
  local copies, waits for them, and re-layouts  5.35 us (5%)
    pallas_call x1, Pallas kernels, per_device(): pl.pallas_call(functools.partial(layer_kernel, n, rounds), grid=(steps,),...  94.5 us
    unnamed x13, local copies, waits for them, and re-layouts  5.35 us

profile of v2, /device:TPU:0, one launch (start us, length us, event | category | flops | bytes accessed | tf_op | source)
XLA Modules:
  0.0 100.5 jit_solution(17147644113351568788)
XLA Ops:
  0.6 94.5 %layer.1 = (bf16[64,4096]{1,0:T(8,128)(2,1)}, bf16[64,4096]{1,0:T(8,128)(2,1)}, bf16[64,4096]{1,0:T(8,128)(2,1)}, bf16[64,4096]{1,0:T(8,128)(2,1)}, bf16[32,64]{1,0:T(8,128)(2,1)}) custom-call(bf16[64,4096]{1,0:T(8,128)(2,1)} %q_ref.1, bf16[64,4096]{1,0:T(8,128)(2,1)} %k_ref.1, bf16[64,4096]{1,0:T(8,128)(2,1)} %v_ref.1, bf16[64,4096]{1,0:T(8,128)(2,1)} %g_ref.1, ...), custom_call_target="tpu_custom_call" | custom-call | tf_op jit(solution)/shard_map/layer/pallas_call | solution.py:698
  95.1 0.0 copy-start.2
  95.1 1.9 %copy.16 = bf16[64,4096]{1,0:T(8,128)(2,1)} copy(bf16[64,4096]{1,0:T(8,128)(2,1)} %get-tuple-element.20) | data formatting | bytes 1048576
  97.1 0.0 copy-done.2
  97.1 0.0 copy-start.1
  97.1 0.8 copy.17
  97.9 0.4 copy-done.1
  98.3 0.0 copy-start.3
  98.3 0.0 copy-start
  98.3 0.8 copy.18
  99.1 0.0 copy-done.3
  99.1 0.6 copy.19
  99.7 0.0 copy-done
  99.7 0.8 copy.20
Async XLA Ops:
  95.1 1.9 %copy-start.2 = (bf16[64,4096]{1,0:T(8,128)(2,1)S(1)}, bf16[64,4096]{1,0:T(8,128)(2,1)}, u32[]{:S(2)}) copy-start(bf16[64,4096]{1,0:T(8,128)(2,1)} %get-tuple-element.21) | copy-start | bytes 1572868
  97.1 1.2 %copy-start.1 = (bf16[64,4096]{1,0:T(8,128)(2,1)S(1)}, bf16[64,4096]{1,0:T(8,128)(2,1)}, u32[]{:S(2)}) copy-start(bf16[64,4096]{1,0:T(8,128)(2,1)} %get-tuple-element.22) | copy-start | bytes 1572868
  98.3 0.8 copy-start.3
  98.3 1.4 %copy-start = (bf16[64,4096]{1,0:T(8,128)(2,1)S(1)}, bf16[64,4096]{1,0:T(8,128)(2,1)}, u32[]{:S(2)}) copy-start(bf16[64,4096]{1,0:T(8,128)(2,1)} %get-tuple-element.24) | copy-start | bytes 1572868

commit v3 on v2

--- a/solution.py
+++ b/solution.py
@@ -9,9 +9,10 @@
 
 GROUP = 2
 HOP = 3
-SWAP = 4
-NEAR = 2
-EVERY = 2
+SWAP = 3
+NEAR = 1
+FAR = 2
+EVERY = 3
 BACK = 4
 BATCH = 4
 BASE = 2
@@ -192,9 +193,9 @@
     diagonal = small_row == small_col
     for u in range(units):
         g = first + u
-        a_ref[g] = inners[u]
-        sc_ref[g] = scores[u]
-        inv_ref[g] = founds[u]
+        a_ref[g] = inners[u].T
+        sc_ref[g] = scores[u].T
+        inv_ref[g] = founds[u].T
         ev_ref[g] = e_values[u]
         ek_ref[g] = e_keys[u]
     for j in range(count):
@@ -221,9 +222,9 @@
     numbers = [first + u for u in range(units)]
     states = [[ends[g, j, 0] for j in spans] for g in numbers]
     grads = [[ends[g, j, 1] for j in spans] for g in numbers]
-    scores_t = [sc_ref[g].T for g in numbers]
-    inner_t = [a_ref[g].T for g in numbers]
-    found_t = [inv_ref[g].T for g in numbers]
+    scores_t = [sc_ref[g] for g in numbers]
+    inner_t = [a_ref[g] for g in numbers]
+    found_t = [inv_ref[g] for g in numbers]
     e_values = [ev_ref[g] for g in numbers]
     e_keys = [ek_ref[g] for g in numbers]
 
@@ -343,8 +344,8 @@
     reduce_at = [HOP * s for s in range(n)]
     scan_at = []
     for r in range(rounds):
-        near = r == 0 or r == rounds - 1
-        scan_at.append((scan_at[-1] if r else reduce_at[-1]) + (NEAR if near else SWAP))
+        slack = NEAR if r == 0 else FAR if r == rounds - 1 else SWAP
+        scan_at.append((scan_at[-1] if r else reduce_at[-1]) + slack)
     back_at = [scan_at[-1] + BACK * b for b in range(n)]
     return reduce_at, scan_at, back_at, back_at[-1] + 1
 
@@ -429,7 +430,6 @@
         for r in range(rounds):
             pl.semaphore_signal(barrier, inc=1, device_id={"ctx": partner(r)}, device_id_type=MESH)
         db_all[...] = jnp.zeros_like(db_all)
-        pl.semaphore_wait(barrier, rounds + jnp.where(z > 0, 1, 0) + jnp.where(z < n - 1, 1, 0))
         pltpu.make_async_copy(b_ref, table, table_sem).wait()
 
     def own(g, j):
@@ -459,6 +459,11 @@
         for index in range(len(ins)):
             load(index, batch).wait()
         local_part(batch, units, count, held, table, saved, tags)
+
+        @pl.when(t == 0)
+        def _():
+            barrier = pltpu.get_barrier_semaphore()
+            pl.semaphore_wait(barrier, rounds + jnp.where(z > 0, 1, 0) + jnp.where(z < n - 1, 1, 0))
 
         @pl.when(z == 0)
         def _():
@@ -671,6 +676,35 @@
 
         lax.fori_loop(0, batches, finish_batch, 0)
         db_copy.wait()
+
+
+def copy_kernel(*refs):
+    total = len(refs) - 2
+    arrays = total // 3
+    sources, targets, buffers = refs[:arrays], refs[arrays : 2 * arrays], refs[2 * arrays : total]
+    in_sem, out_sem = refs[total:]
+    fetch = [pltpu.make_async_copy(x, y, in_sem.at[i]) for i, (x, y) in enumerate(zip(sources, buffers))]
+    put = [pltpu.make_async_copy(x, y, out_sem.at[i]) for i, (x, y) in enumerate(zip(buffers, targets))]
+    for copy in fetch:
+        copy.start()
+    for first, second in zip(fetch, put):
+        first.wait()
+        second.start()
+    for copy in put:
+        copy.wait()
+
+
+def placed(arrays):
+    outside = pl.BlockSpec(memory_space=pl.ANY)
+    count = len(arrays)
+    return pl.pallas_call(
+        copy_kernel,
+        in_specs=[outside] * count,
+        out_specs=[outside] * count,
+        out_shape=[jax.ShapeDtypeStruct(x.shape, x.dtype) for x in arrays],
+        scratch_shapes=[pltpu.VMEM(x.shape, x.dtype) for x in arrays] + [pltpu.SemaphoreType.DMA((count,))] * 2,
+        name="place",
+    )(*arrays)
 
 
 def per_device(queries, key_in, values_in, strength, log_decay, d_out):
@@ -717,6 +751,7 @@
         ),
         name="layer",
     )(queries, key_in, values_in, log_decay, d_out, strength.T)
+    dq, dk, dv, dg, ds = placed([dq, dk, dv, dg, ds])
     return dq, dk, dv, ds.T, dg
 
 

time: 101 us -> 94 us (0.931)
  local copies, waits for them, and re-layouts: 5.35 us -> 0 us
  Pallas kernels: 94.5 us -> 93.2 us
    unnamed x13 -> x0, local copies, waits for them, and re-layouts: 5.35 us -> none
    pallas_call x1, Pallas kernels: 94.5 us -> 90.8 us  [per_device(): pl.pallas_call(functools.partial(layer_kernel, n, rounds), grid=(steps,),...]
    pallas_call x0 -> x1, Pallas kernels: none -> 2.44 us  [placed(): pl.pallas_call(copy_kernel, in_specs=[outside] * count, out_specs=[outsid...]
where the time goes in v3:
time: 94 us; the launch traced here: 93.9 us
  Pallas kernels  93.2 us (99%)
    pallas_call x1, Pallas kernels, per_device(): pl.pallas_call(functools.partial(layer_kernel, n, rounds), grid=(steps,),...  90.8 us
    pallas_call x1, Pallas kernels, placed(): pl.pallas_call(copy_kernel, in_specs=[outside] * count, out_specs=[outsid...  2.44 us

profile of v3, /device:TPU:0, one launch (start us, length us, event | category | flops | bytes accessed | tf_op | source)
XLA Modules:
  0.0 93.9 jit_solution(9898728646049114229)
XLA Ops:
  0.6 90.8 %layer.1 = (bf16[64,4096]{1,0:T(8,128)(2,1)}, bf16[64,4096]{1,0:T(8,128)(2,1)}, bf16[64,4096]{1,0:T(8,128)(2,1)}, bf16[64,4096]{1,0:T(8,128)(2,1)}, bf16[32,64]{1,0:T(8,128)(2,1)}) custom-call(bf16[64,4096]{1,0:T(8,128)(2,1)} %q_ref.1, bf16[64,4096]{1,0:T(8,128)(2,1)} %k_ref.1, bf16[64,4096]{1,0:T(8,128)(2,1)} %v_ref.1, bf16[64,4096]{1,0:T(8,128)(2,1)} %g_ref.1, ...), custom_call_target="tpu_custom_call" | custom-call | tf_op jit(solution)/shard_map/layer/pallas_call | solution.py:732
  91.4 2.4 %place.1 = (bf16[64,4096]{1,0:T(8,128)(2,1)}, bf16[64,4096]{1,0:T(8,128)(2,1)}, bf16[64,4096]{1,0:T(8,128)(2,1)}, bf16[64,4096]{1,0:T(8,128)(2,1)}, bf16[32,64]{1,0:T(8,128)(2,1)}) custom-call(bf16[64,4096]{1,0:T(8,128)(2,1)} %get-tuple-element.15.refs_0_, bf16[64,4096]{1,0:T(8,128)(2,1)} %get-tuple-element.16.refs_1_, ...), custom_call_target="tpu_custom_call" | custom-call | tf_op jit(solution)/shard_map/place/pallas_call | solution.py:700

commit v4 on v3

--- a/solution.py
+++ b/solution.py
@@ -347,7 +347,7 @@
         slack = NEAR if r == 0 else FAR if r == rounds - 1 else SWAP
         scan_at.append((scan_at[-1] if r else reduce_at[-1]) + slack)
     back_at = [scan_at[-1] + BACK * b for b in range(n)]
-    return reduce_at, scan_at, back_at, back_at[-1] + 1
+    return reduce_at, scan_at, back_at, back_at[-1]
 
 
 def layer_kernel(n, rounds, q_ref, k_ref, v_ref, g_ref, o_ref, b_ref, dq_out, dk_out, dv_out, dg_out, db_out,
@@ -630,13 +630,13 @@
     def _():
         local_stage(t // EVERY)
 
-    at_batch(grad_at + units - 1, grad_stage)
+    for s in range(n - 1, 0, -1):
+        at(reduce_at[s], functools.partial(reduce_stage, s))
     for b in range(n - 1, 0, -1):
         at(back_at[b], functools.partial(back_stage, b))
     for r in range(rounds - 1, -1, -1):
         at(scan_at[r], functools.partial(scan_stage, r))
-    for s in range(n - 1, 0, -1):
-        at(reduce_at[s], functools.partial(reduce_stage, s))
+    at_batch(grad_at + units - 1, grad_stage)
 
     @pl.when(t == groups + grad_at - 1)
     def _():

time: 94 us -> 95.6 us (1.017)
  Pallas kernels: 93.2 us -> 94.8 us
    pallas_call x1, Pallas kernels: 90.8 us -> 92.4 us  [per_device(): pl.pallas_call(functools.partial(layer_kernel, n, rounds), grid=(steps,),...]
where the time goes in v4:
time: 95.6 us; the launch traced here: 95.5 us
  Pallas kernels  94.8 us (99%)
    pallas_call x1, Pallas kernels, per_device(): pl.pallas_call(functools.partial(layer_kernel, n, rounds), grid=(steps,),...  92.4 us
    pallas_call x1, Pallas kernels, placed(): pl.pallas_call(copy_kernel, in_specs=[outside] * count, out_specs=[outsid...  2.44 us

profile of v4, /device:TPU:0, one launch (start us, length us, event | category | flops | bytes accessed | tf_op | source)
XLA Modules:
  0.0 95.5 jit_solution(7968857327133600651)
XLA Ops:
  0.6 92.4 %layer.1 = (bf16[64,4096]{1,0:T(8,128)(2,1)}, bf16[64,4096]{1,0:T(8,128)(2,1)}, bf16[64,4096]{1,0:T(8,128)(2,1)}, bf16[64,4096]{1,0:T(8,128)(2,1)}, bf16[32,64]{1,0:T(8,128)(2,1)}) custom-call(bf16[64,4096]{1,0:T(8,128)(2,1)} %q_ref.1, bf16[64,4096]{1,0:T(8,128)(2,1)} %k_ref.1, bf16[64,4096]{1,0:T(8,128)(2,1)} %v_ref.1, bf16[64,4096]{1,0:T(8,128)(2,1)} %g_ref.1, ...), custom_call_target="tpu_custom_call" | custom-call | tf_op jit(solution)/shard_map/layer/pallas_call | solution.py:732
  93.0 2.4 %place.1 = (bf16[64,4096]{1,0:T(8,128)(2,1)}, bf16[64,4096]{1,0:T(8,128)(2,1)}, bf16[64,4096]{1,0:T(8,128)(2,1)}, bf16[64,4096]{1,0:T(8,128)(2,1)}, bf16[32,64]{1,0:T(8,128)(2,1)}) custom-call(bf16[64,4096]{1,0:T(8,128)(2,1)} %get-tuple-element.15.refs_0_, bf16[64,4096]{1,0:T(8,128)(2,1)} %get-tuple-element.16.refs_1_, ...), custom_call_target="tpu_custom_call" | custom-call | tf_op jit(solution)/shard_map/place/pallas_call | solution.py:700
